TPU v7x, 32 devices: a whole 2x2x4 slice. The times are simulated.
32 devices in a mesh: parts: 2 (over y), rows: 4 (over z), ex: 4 (over x, core).
Axes of the slice: x: 2, y: 2, z: 4, core: 2. Of those that a mesh axis runs over, the one named last changes fastest.
Arguments:
- hidden_acts: bfloat16 [1024, 512], P(('parts', 'ex'), 'rows'), parts along dimension 0, may hold values from -6 to 6
- cotangent: bfloat16 [1024, 4096], P(('parts', 'ex'), 'rows'), parts along dimension 0, may hold values from -0.796875 to 0.796875
- lengths: int32 [64], P('parts'), parts along dimension 0, may hold values from 1 to 64, 512 in all
- row_signs: int32 [512], P('rows'), may hold values from -1 to 1, as said below
- col_signs: int32 [4096], replicated, may hold values from -1 to 1, as said below
- feat_row: int32 [8192], replicated, may hold values from 0 to 511
- feat_col: int32 [8192], replicated, may hold values from 0 to 4095
- inverse_rows: bfloat16 [8192, 8192], P('rows'), as said below
Outputs:
- scores: bfloat16 [64, 8192], P(('parts', 'ex'), 'rows'), parts along dimension 0
There are 2 independent parts, one for each index of `parts`. A program takes and returns all parts, laid end to end along the dimension named above; an argument that names none is the same for every part. Nothing has to cross between parts.
Inputs may be any that keep to these rules, and one draw needn't show every extreme that they name: `row_signs`: every entry is -1 or +1. `col_signs`: every entry is -1 or +1. `inverse_rows`: the whole matrix equals its transpose. The lengths sum to 512 and the largest equals 64.
All inputs are finite; a program needn't handle non-finite values.
Results may differ from a plain program's by a relative error of at most 0.0049.
Values may be sent and summed in bfloat16 or wider, within the bound.
A program may use at most 128 MiB of HBM per device.

v0:
```python
import functools
import math

import jax
import jax.numpy as jnp
from jax import lax
from jax.experimental import pallas as pl
from jax.experimental.pallas import tpu as pltpu
from jax.sharding import PartitionSpec as P


def signs(first_bits, second_bits):
    odd = lax.population_count(first_bits & second_bits) & 1
    return (1 - 2 * odd).astype(jnp.float32).astype(jnp.bfloat16)


def sign_rows(first, count, step, picks):
    inner = lax.broadcasted_iota(jnp.int32, (step, picks.shape[1]), 0)
    table = signs(inner, picks)
    parts = [table * signs(jnp.zeros_like(picks) + (first + n * step), picks) for n in range(count)]
    return parts[0] if count == 1 else jnp.concatenate(parts, axis=0)


def loop(count, body):
    if count <= 4:
        for n in range(count):
            body(n)
    else:
        lax.fori_loop(0, count, lambda n, c: (body(n), c)[1], 0)


def when(cond, body):
    if isinstance(cond, bool):
        if cond:
            body()
    else:
        pl.when(cond)(body)


def kernel(
    row_count,
    ex_count,
    norm_scale,
    hid_ref,
    cot_ref,
    len_ref,
    rsign_ref,
    csign_ref,
    frow_ref,
    fcol_ref,
    inv_ref,
    out_ref,
    hid_all,
    cot_signed,
    right_buf,
    part_buf,
    ex_in,
    row_out,
    row_in,
    score_out,
    score_in,
    inv_buf,
    total_buf,
    inv_sem,
    hid_send,
    hid_recv,
    ex_send,
    ex_recv,
    row_send,
    row_recv,
    score_send,
    score_recv,
):
    row = lax.axis_index("rows")
    ex = lax.axis_index("ex")
    tok_dev, width = hid_ref.shape
    cot_width = cot_ref.shape[1]
    features = frow_ref.shape[1]
    own = features // row_count
    examples = len_ref.shape[1]
    chunk = min(own, 512)
    ex_steps = ex_count.bit_length() - 1

    def block_of(i):
        return lax.rem(row + 1 + i, row_count)

    def inv_copy(n):
        cols = pl.ds(pl.multiple_of(block_of(n) * own, 128), own)
        return pltpu.make_async_copy(inv_ref.at[:, cols], inv_buf.at[n], inv_sem.at[n])

    barrier = pltpu.get_barrier_semaphore()

    def greet(n):
        pl.semaphore_signal(
            barrier,
            inc=1,
            device_id={"rows": lax.rem(row + n + 1, row_count)},
            device_id_type=pl.DeviceIdType.MESH,
        )

    loop(row_count - 1, greet)

    def bit_of(step):
        return lax.rem(ex // (1 << step), 2)

    def partner_of(step):
        return ex + (1 - 2 * bit_of(step)) * (1 << step)

    for step in range(ex_steps):
        pl.semaphore_signal(
            barrier,
            inc=1,
            device_id={"ex": partner_of(step)},
            device_id_type=pl.DeviceIdType.MESH,
        )
    loop(row_count, lambda n: inv_copy(n).start())
    hid_all[row] = hid_ref[...] * rsign_ref[...].astype(jnp.float32).astype(jnp.bfloat16)
    if csign_ref.shape[1] == cot_width:
        col_sign = csign_ref[...]
    else:
        col_sign = csign_ref[:, pl.ds(pl.multiple_of(row * cot_width, 128), cot_width)]
    cot_signed[...] = cot_ref[...] * col_sign.astype(jnp.float32).astype(jnp.bfloat16)
    lens = jnp.broadcast_to(len_ref[...].astype(jnp.float32), (examples, examples))
    e_row = lax.broadcasted_iota(jnp.int32, (examples, examples), 0)
    e_col = lax.broadcasted_iota(jnp.int32, (examples, examples), 1)
    ends = jnp.sum(jnp.where(e_col <= e_row, lens, 0.0), axis=1, keepdims=True)
    starts = jnp.sum(jnp.where(e_col < e_row, lens, 0.0), axis=1, keepdims=True)
    spots = ex * tok_dev + lax.broadcasted_iota(jnp.int32, (examples, tok_dev), 1)
    spots = spots.astype(jnp.float32)
    member = jnp.where((spots >= starts) & (spots < ends), 1.0, 0.0).astype(jnp.bfloat16)
    pl.semaphore_wait(barrier, row_count - 1 + ex_steps)

    def hid_copy(n, incoming=False):
        to = lax.rem(row + n + 1, row_count)
        block = lax.rem(row - n - 1 + row_count, row_count) if incoming else row
        return pltpu.make_async_remote_copy(
            src_ref=hid_all.at[block],
            dst_ref=hid_all.at[block],
            send_sem=hid_send.at[n],
            recv_sem=hid_recv.at[n],
            device_id={"rows": to},
            device_id_type=pl.DeviceIdType.MESH,
        )

    loop(row_count - 1, lambda n: hid_copy(n).start())

    def picks_of(ref, i, c):
        at = pl.multiple_of(block_of(i) * own + c * chunk, 128)
        return ref[:, pl.ds(at, chunk)]

    inner = min(cot_width, 128)

    def right_side(i):
        def one(c):
            table = sign_rows(row * cot_width, cot_width // inner, inner, picks_of(fcol_ref, i, c))
            at = c * chunk if isinstance(c, int) else pl.multiple_of(c * chunk, 128)
            right_buf[i, :, pl.ds(at, chunk)] = jnp.dot(
                cot_signed[...], table, preferred_element_type=jnp.float32
            )

        loop(own // chunk, one)

    group = min(row_count, 4)

    def features_of(i):
        def one(c):
            picks = picks_of(frow_ref, i, c)

            def some(g, left):
                acts = jnp.concatenate([hid_all[g * group + n] for n in range(group)], axis=1)
                table = sign_rows(g * group * width, group, width, picks)
                return left + jnp.dot(acts, table, preferred_element_type=jnp.float32)

            left = jnp.zeros((tok_dev, chunk), jnp.float32)
            if row_count == group:
                left = some(0, left)
            else:
                left = lax.fori_loop(0, row_count // group, some, left)
            at = c * chunk if isinstance(c, int) else pl.multiple_of(c * chunk, 128)
            products = left * right_buf[i, :, pl.ds(at, chunk)]
            high = products.astype(jnp.bfloat16)
            rest = (products - high.astype(jnp.float32)).astype(jnp.bfloat16)
            sums = jnp.dot(member, high, preferred_element_type=jnp.float32)
            sums = sums + jnp.dot(member, rest, preferred_element_type=jnp.float32)
            part_buf[i, :, :, pl.ds(at, chunk)] = sums.reshape(ex_count, examples // ex_count, chunk)

        loop(own // chunk, one)

    def ex_copies(i, step):
        size = 1 << step
        first = ex_count - (ex_count >> step)
        copies = []
        for m in range(ex_count >> (step + 1)):
            away = lax.rem(ex, size) + (1 - bit_of(step)) * size + m * 2 * size
            slot = first + m
            copies.append(
                pltpu.make_async_remote_copy(
                    src_ref=part_buf.at[i, away],
                    dst_ref=ex_in.at[i, slot],
                    send_sem=ex_send.at[i, slot],
                    recv_sem=ex_recv.at[i, slot],
                    device_id={"ex": partner_of(step)},
                    device_id_type=pl.DeviceIdType.MESH,
                )
            )
        return copies

    def ex_start(i, step):
        for copy in ex_copies(i, step):
            copy.start()

    def ex_finish(i, step):
        size = 1 << step
        first = ex_count - (ex_count >> step)
        for m, copy in enumerate(ex_copies(i, step)):
            copy.wait_recv()
            mine = lax.rem(ex, 2 * size) + m * 2 * size
            part_buf[i, mine] = part_buf[i, mine] + ex_in[i, first + m]

    def row_copy(i):
        return pltpu.make_async_remote_copy(
            src_ref=row_out.at[i],
            dst_ref=row_in.at[i],
            send_sem=row_send.at[i],
            recv_sem=row_recv.at[i],
            device_id={"rows": block_of(i)},
            device_id_type=pl.DeviceIdType.MESH,
        )

    def stage(i, step):
        def work():
            if step > 0:
                ex_finish(i, step - 1)
            if step < ex_steps:
                ex_start(i, step)
            else:


                def send():
                    row_out[i] = part_buf[i, ex].astype(row_out.dtype)
                    row_copy(i).start()

                when(i < row_count - 1, send)

        return work

    loop(row_count, right_side)
    loop(row_count - 1, lambda n: hid_copy(n, True).wait_recv())

    def block_step(i):
        features_of(i)
        stage(i, 0)()
        for step in range(1, ex_steps + 1):
            when(i >= step, stage(i - step, step))

    loop(row_count, block_step)
    for late in range(1, ex_steps + 1):
        for step in range(late, ex_steps + 1):
            if row_count - 1 + late - step >= 0:
                stage(row_count - 1 + late - step, step)()

    total_buf[...] = part_buf[row_count - 1, ex]

    def add_row(n):
        row_copy(n).wait_recv()
        total_buf[...] = total_buf[...] + row_in[n].astype(jnp.float32)

    loop(row_count - 1, add_row)
    low = (total_buf[...] * norm_scale).astype(jnp.bfloat16)

    def score_copy(n):
        return pltpu.make_async_remote_copy(
            src_ref=score_out.at[n],
            dst_ref=score_in.at[n],
            send_sem=score_send.at[n],
            recv_sem=score_recv.at[n],
            device_id={"rows": block_of(n)},
            device_id_type=pl.DeviceIdType.MESH,
        )

    tile = min(own, 512)

    def score_block(n):
        inv_copy(n).wait()

        def one(j):
            at = j * tile if isinstance(j, int) else pl.multiple_of(j * tile, 128)
            got = jnp.dot(low, inv_buf[n, :, pl.ds(at, tile)], preferred_element_type=jnp.float32)

            def keep():
                total_buf[:, pl.ds(at, tile)] = got

            def give():
                score_out[n, :, pl.ds(at, tile)] = got.astype(score_out.dtype)

            when(n == row_count - 1, keep)
            when(n < row_count - 1, give)

        loop(own // tile, one)
        when(n < row_count - 1, lambda: score_copy(n).start())

    loop(row_count, score_block)
    def add_score(n):
        score_copy(n).wait_recv()
        total_buf[...] = total_buf[...] + score_in[n].astype(jnp.float32)

    loop(row_count - 1, add_score)
    out_ref[...] = total_buf[...].astype(out_ref.dtype)
    loop(row_count - 1, lambda n: hid_copy(n).wait_send())
    loop(row_count - 1, lambda n: score_copy(n).wait_send())
    loop(row_count - 1, lambda n: row_copy(n).wait_send())

    def ex_sent(i):
        for step in range(ex_steps):
            for copy in ex_copies(i, step):
                copy.wait_send()

    loop(row_count, ex_sent)


def local(hidden_acts, cotangent, lengths, row_signs, col_signs, feat_row, feat_col, inverse_rows):
    row_count = lax.axis_size("rows")
    ex_count = lax.axis_size("ex")
    tok_dev, width = hidden_acts.shape
    cot_width = cotangent.shape[1]
    features = feat_row.shape[0]
    examples = lengths.shape[0]
    own = features // row_count
    owned = examples // ex_count
    norm_scale = 1.0 / math.sqrt(width * row_count * col_signs.shape[0])
    if cot_width % 128 != 0:
        col_signs = lax.dynamic_slice(col_signs, (lax.axis_index("rows") * cot_width,), (cot_width,))
    vmem = pl.BlockSpec(memory_space=pltpu.VMEM)
    others = max(row_count - 1, 1)
    dma = pltpu.SemaphoreType.DMA
    return pl.pallas_call(
        functools.partial(kernel, row_count, ex_count, norm_scale),
        out_shape=jax.ShapeDtypeStruct((owned, own), jnp.bfloat16),
        in_specs=[vmem] * 7 + [pl.BlockSpec(memory_space=pl.ANY)],
        out_specs=vmem,
        scratch_shapes=[
            pltpu.VMEM((row_count, tok_dev, width), jnp.bfloat16),
            pltpu.VMEM((tok_dev, cot_width), jnp.bfloat16),
            pltpu.VMEM((row_count, tok_dev, own), jnp.float32),
            pltpu.VMEM((row_count, ex_count, owned, own), jnp.float32),
            pltpu.VMEM((row_count, max(ex_count - 1, 1), owned, own), jnp.float32),
            pltpu.VMEM((others, owned, own), jnp.bfloat16),
            pltpu.VMEM((others, owned, own), jnp.bfloat16),
            pltpu.VMEM((others, owned, own), jnp.bfloat16),
            pltpu.VMEM((others, owned, own), jnp.bfloat16),
            pltpu.VMEM((row_count, own, own), jnp.bfloat16),
            pltpu.VMEM((owned, own), jnp.float32),
            dma((row_count,)),
            dma((others,)),
            dma((others,)),
            dma((row_count, max(ex_count - 1, 1))),
            dma((row_count, max(ex_count - 1, 1))),
            dma((others,)),
            dma((others,)),
            dma((others,)),
            dma((others,)),
        ],
        compiler_params=pltpu.CompilerParams(
            collective_id=0, has_side_effects=True, vmem_limit_bytes=60 * 1024 * 1024
        ),
        name="features_and_scores",
    )(
        hidden_acts,
        cotangent,
        lengths.reshape(1, -1),
        row_signs.reshape(1, -1),
        col_signs.reshape(1, -1),
        feat_row.reshape(1, -1),
        feat_col.reshape(1, -1),
        inverse_rows,
    )


def solution(mesh):
    placed = (
        P(("parts", "ex"), "rows"),
        P(("parts", "ex"), "rows"),
        P("parts"),
        P("rows"),
        P(),
        P(),
        P(),
        P("rows", None),
    )
    return jax.shard_map(
        local, mesh=mesh, in_specs=placed, out_specs=P(("parts", "ex"), "rows"), check_vma=False
    )
```

profile of v0, /device:TPU:0, one launch (start us, length us, event | category | flops | bytes accessed | tf_op | source)
XLA Modules:
  0.0 32.9 jit_solution(11966895490087016586)
XLA Ops:
  0.0 31.5 %features_and_scores.1 = bf16[8,2048]{1,0:T(8,128)(2,1)} custom-call(bf16[128,128]{1,0:T(8,128)(2,1)} %hid_ref.1, bf16[128,1024]{1,0:T(8,128)(2,1)} %cot_ref.1, s32[1,32]{1,0:T(1,128)} %bitcast.8, s32[1,128]{1,0:T(1,128)} %bitcast.9, s32[1,4096]{1,0:T(1,128)} %bitcast.7, s32[1,8192]{1,0:T(1,128)} %bitcast.5, s32[1,8192]{1,0:T(1,128)} %bitcast.6, ...), custom_call_target="tpu_custom_call" | custom-call | tf_op jit(solution)/shard_map/features_and_scores/pallas_call | solution.py:336
  31.5 1.4 %copy.10 = bf16[8,2048]{1,0:T(8,128)(2,1)} copy(bf16[8,2048]{1,0:T(8,128)(2,1)} %features_and_scores.1) | data formatting | bytes 65536
where the time goes:
time: 33.1 us; the launch traced here: 32.9 us
  Pallas kernels  31.5 us (95%)
  local copies, waits for them, and re-layouts  1.38 us (4%)
    pallas_call x1, Pallas kernels, local(): pl.pallas_call(functools.partial(kernel, row_count, ex_count, norm_scale)...  31.5 us
    unnamed x1, local copies, waits for them, and re-layouts  1.38 us

commit v1 on v0

--- a/solution.py
+++ b/solution.py
@@ -318,6 +318,411 @@
     loop(row_count, ex_sent)
 
 
+def pair_kernel(
+    row_count,
+    ex_count,
+    norm_scale,
+    hid_hbm,
+    cot_hbm,
+    len_hbm,
+    rsign_hbm,
+    csign_hbm,
+    frow_hbm,
+    fcol_hbm,
+    inv_ref,
+    out_ref,
+    hid_buf,
+    cot_buf,
+    len_buf,
+    rsign_buf,
+    csign_buf,
+    frow_buf,
+    fcol_buf,
+    hid_all,
+    cot_all,
+    right_table,
+    left_table,
+    right_buf,
+    high_buf,
+    rest_buf,
+    part_buf,
+    ex_out,
+    ex_in,
+    row_out,
+    row_in,
+    keep_buf,
+    mate_buf,
+    score_out,
+    score_in,
+    inv_buf,
+    load_sem,
+    inv_sem,
+    hid_send,
+    hid_recv,
+    relay_send,
+    relay_recv,
+    cot_send,
+    cot_recv,
+    ex_send,
+    ex_recv,
+    row_send,
+    row_recv,
+    mate_send,
+    mate_recv,
+    score_send,
+    score_recv,
+):
+    row = lax.axis_index("rows")
+    ex = lax.axis_index("ex")
+    core = lax.rem(ex, 2)
+    mate = ex + 1 - 2 * core
+    group = ex // 2
+    groups = ex_count // 2
+    tok_dev, width = hid_hbm.shape
+    cot_width = cot_hbm.shape[1]
+    features = frow_hbm.shape[1]
+    own = features // row_count
+    half = own // 2
+    examples = len_hbm.shape[1]
+    chunk = min(half, 512)
+    mesh_id = pl.DeviceIdType.MESH
+    last = row_count - 1
+
+    def other_row(n):
+        far, at = last - n, row
+        for bit in range(row_count.bit_length() - 1):
+            if far >> bit & 1:
+                at = at + (1 - 2 * lax.rem(row // (1 << bit), 2)) * (1 << bit)
+        return at
+
+    def other_group(n):
+        return lax.rem(group + 1 + n, groups)
+
+    barrier = pltpu.get_barrier_semaphore()
+    for n in range(last):
+        pl.semaphore_signal(barrier, inc=1, device_id={"rows": other_row(n)}, device_id_type=mesh_id)
+    for n in range(groups - 1):
+        pl.semaphore_signal(
+            barrier, inc=1, device_id={"ex": 2 * other_group(n) + core}, device_id_type=mesh_id
+        )
+    pl.semaphore_signal(barrier, inc=1, device_id={"ex": mate}, device_id_type=mesh_id)
+
+    cols = pl.ds(pl.multiple_of(row * cot_width, 128), cot_width)
+    loads = {
+        name: pltpu.make_async_copy(source, target, load_sem.at[n])
+        for n, (name, source, target) in enumerate(
+            (
+                ("hid", hid_hbm, hid_buf),
+                ("rsign", rsign_hbm, rsign_buf),
+                ("cot", cot_hbm, cot_buf),
+                ("csign", csign_hbm.at[:, cols], csign_buf),
+                ("fcol", fcol_hbm, fcol_buf),
+                ("frow", frow_hbm, frow_buf),
+                ("len", len_hbm, len_buf),
+            )
+        )
+    }
+    for load in loads.values():
+        load.start()
+
+    def inv_copy(n):
+        target = pl.ds(pl.multiple_of(other_row(n) * own, 128), own)
+        source = pl.ds(pl.multiple_of(core * half, 16), half)
+        return pltpu.make_async_copy(inv_ref.at[source, target], inv_buf.at[n], inv_sem.at[n])
+
+    def picks_of(ref, i, c):
+        at = pl.multiple_of(other_row(i) * own + core * half + c * chunk, 128)
+        return ref[:, pl.ds(at, chunk)]
+
+    def spot(i, c):
+        return slice(i * half + c * chunk, i * half + (c + 1) * chunk)
+
+    inner = min(cot_width, 128)
+
+    loads["hid"].wait()
+    loads["rsign"].wait()
+    hid_all[core, row] = hid_buf[...] * rsign_buf[...].astype(jnp.float32).astype(jnp.bfloat16)
+    loads["cot"].wait()
+    loads["csign"].wait()
+    cot_all[core] = cot_buf[...] * csign_buf[...].astype(jnp.float32).astype(jnp.bfloat16)
+    loads["fcol"].wait()
+
+    def right_first(i):
+        for c in range(half // chunk):
+            table = sign_rows(row * cot_width, cot_width // inner, inner, picks_of(fcol_buf, i, c))
+            right_table[:, spot(i, c)] = table
+            right_buf[core, :, spot(i, c)] = jnp.dot(
+                cot_all[core], table, preferred_element_type=jnp.float32
+            )
+
+    def right_mate(i):
+        for c in range(half // chunk):
+            right_buf[1 - core, :, spot(i, c)] = jnp.dot(
+                cot_all[1 - core], right_table[:, spot(i, c)], preferred_element_type=jnp.float32
+            )
+
+    def hid_copy(n, block):
+        return pltpu.make_async_remote_copy(
+            src_ref=hid_all.at[core, block],
+            dst_ref=hid_all.at[core, block],
+            send_sem=hid_send.at[n],
+            recv_sem=hid_recv.at[n],
+            device_id={"rows": other_row(n)},
+            device_id_type=mesh_id,
+        )
+
+    def relay_copy(n, side):
+        return pltpu.make_async_remote_copy(
+            src_ref=hid_all.at[side, other_row(n)],
+            dst_ref=hid_all.at[side, other_row(n)],
+            send_sem=relay_send.at[n],
+            recv_sem=relay_recv.at[n],
+            device_id={"ex": mate},
+            device_id_type=mesh_id,
+        )
+
+    def cot_copy(side):
+        return pltpu.make_async_remote_copy(
+            src_ref=cot_all.at[side],
+            dst_ref=cot_all.at[side],
+            send_sem=cot_send,
+            recv_sem=cot_recv,
+            device_id={"ex": mate},
+            device_id_type=mesh_id,
+        )
+
+    early = row_count // 2
+    for i in range(early):
+        right_first(i)
+    pl.semaphore_wait(barrier, last + groups)
+    for n in range(last):
+        hid_copy(n, row).start()
+    relay_copy(last, core).start()
+    cot_copy(core).start()
+
+    loads["len"].wait()
+    lens = jnp.broadcast_to(len_buf[...].astype(jnp.float32), (examples, examples))
+    e_row = lax.broadcasted_iota(jnp.int32, (examples, examples), 0)
+    e_col = lax.broadcasted_iota(jnp.int32, (examples, examples), 1)
+    ends = jnp.sum(jnp.where(e_col <= e_row, lens, 0.0), axis=1, keepdims=True)
+    starts = jnp.sum(jnp.where(e_col < e_row, lens, 0.0), axis=1, keepdims=True)
+
+    spots = 2 * group * tok_dev + lax.broadcasted_iota(jnp.int32, (examples, 2 * tok_dev), 1)
+    spots = spots.astype(jnp.float32)
+    member = jnp.where((spots >= starts) & (spots < ends), 1.0, 0.0).astype(jnp.bfloat16)
+
+    for i in range(early, row_count):
+        right_first(i)
+    loads["frow"].wait()
+    for i in range(row_count):
+        for c in range(half // chunk):
+            left_table[:, spot(i, c)] = sign_rows(0, row_count, width, picks_of(frow_buf, i, c))
+
+    cot_copy(1 - core).wait_recv()
+    for i in range(row_count):
+        right_mate(i)
+
+    for n in range(last):
+        hid_copy(n, other_row(n)).wait_recv()
+        relay_copy(n, core).start()
+    for n in range(row_count):
+        inv_copy(n).start()
+
+    def products_of(side, tokens):
+        acts = jnp.concatenate([hid_all[side, n] for n in range(row_count)], axis=1)
+        for i in range(row_count):
+            for c in range(half // chunk):
+                left = jnp.dot(acts, left_table[:, spot(i, c)], preferred_element_type=jnp.float32)
+                products = left * right_buf[side, :, spot(i, c)]
+                high = products.astype(jnp.bfloat16)
+                high_buf[tokens, spot(i, c)] = high
+                rest_buf[tokens, spot(i, c)] = (products - high.astype(jnp.float32)).astype(jnp.bfloat16)
+
+    own_tokens = pl.ds(pl.multiple_of(core * tok_dev, 16), tok_dev)
+    mate_tokens = pl.ds(pl.multiple_of((1 - core) * tok_dev, 16), tok_dev)
+    products_of(core, own_tokens)
+    for n in range(row_count):
+        relay_copy(n, 1 - core).wait_recv()
+    products_of(1 - core, mate_tokens)
+
+    def ex_copy(i, n):
+        return pltpu.make_async_remote_copy(
+            src_ref=ex_out.at[i, n],
+            dst_ref=ex_in.at[i, n],
+            send_sem=ex_send.at[i, n],
+            recv_sem=ex_recv.at[i, n],
+            device_id={"ex": 2 * other_group(n) + core},
+            device_id_type=mesh_id,
+        )
+
+    def row_copy(i):
+        return pltpu.make_async_remote_copy(
+            src_ref=row_out.at[i],
+            dst_ref=row_in.at[i],
+            send_sem=row_send.at[i],
+            recv_sem=row_recv.at[i],
+            device_id={"rows": other_row(i)},
+            device_id_type=mesh_id,
+        )
+
+    def sums_of(i):
+        at = slice(i * half, (i + 1) * half)
+        sums = jnp.dot(member, high_buf[:, at], preferred_element_type=jnp.float32)
+        return sums + jnp.dot(member, rest_buf[:, at], preferred_element_type=jnp.float32)
+
+    def ex_start(i, sums):
+        part_buf[i] = sums.reshape(groups, examples // groups, half)
+        for n in range(groups - 1):
+            ex_out[i, n] = part_buf[i, other_group(n)].astype(ex_out.dtype)
+            ex_copy(i, n).start()
+
+    ready = sums_of(0)
+    for i in range(1, row_count):
+        later = sums_of(i)
+        ex_start(i - 1, ready)
+        ready = later
+    ex_start(last, ready)
+
+    total = None
+    for i in range(row_count):
+        total = part_buf[i, group]
+        for n in range(groups - 1):
+            ex_copy(i, n).wait_recv()
+            total = total + ex_in[i, n].astype(jnp.float32)
+        if i < last:
+            row_out[i] = total.astype(row_out.dtype)
+            row_copy(i).start()
+    for n in range(last):
+        row_copy(n).wait_recv()
+        total = total + row_in[n].astype(jnp.float32)
+    low = (total * norm_scale).astype(jnp.bfloat16)
+
+    def mate_copy(n):
+        return pltpu.make_async_remote_copy(
+            src_ref=keep_buf.at[n, 1 - core],
+            dst_ref=mate_buf.at[n],
+            send_sem=mate_send.at[n],
+            recv_sem=mate_recv.at[n],
+            device_id={"ex": mate},
+            device_id_type=mesh_id,
+        )
+
+    def score_copy(n):
+        return pltpu.make_async_remote_copy(
+            src_ref=score_out.at[n],
+            dst_ref=score_in.at[n],
+            send_sem=score_send.at[n],
+            recv_sem=score_recv.at[n],
+            device_id={"rows": other_row(n)},
+            device_id_type=mesh_id,
+        )
+
+    tile = min(own, 512)
+    owned = examples // ex_count
+
+    def score_block(n):
+        inv_copy(n).wait()
+        for j in range(own // tile):
+            at = slice(j * tile, (j + 1) * tile)
+            got = jnp.dot(low, inv_buf[n, :, at], preferred_element_type=jnp.float32)
+            keep_buf[n, :, :, at] = got.reshape(2, owned, tile)
+        mate_copy(n).start()
+
+    def score_sum(n):
+        mate_copy(n).wait_recv()
+        return keep_buf[n, core] + mate_buf[n]
+
+    for n in range(row_count):
+        score_block(n)
+        if n >= 1:
+            score_out[n - 1] = score_sum(n - 1).astype(score_out.dtype)
+            score_copy(n - 1).start()
+    total = score_sum(last)
+    for n in range(last):
+        score_copy(n).wait_recv()
+        total = total + score_in[n].astype(jnp.float32)
+    out_ref[...] = total.astype(out_ref.dtype)
+
+    cot_copy(core).wait_send()
+    for n in range(row_count):
+        relay_copy(n, core).wait_send()
+        mate_copy(n).wait_send()
+        for m in range(groups - 1):
+            ex_copy(n, m).wait_send()
+    for n in range(last):
+        hid_copy(n, row).wait_send()
+        row_copy(n).wait_send()
+        score_copy(n).wait_send()
+
+
+def pair_call(row_count, ex_count, norm_scale, operands):
+    hidden_acts, cotangent, lengths, frow = operands[0], operands[1], operands[2], operands[5]
+    tok_dev, width = hidden_acts.shape
+    cot_width = cotangent.shape[1]
+    examples = lengths.shape[1]
+    features = frow.shape[1]
+    own = features // row_count
+    half = own // 2
+    groups = ex_count // 2
+    owned = examples // ex_count
+    last, others = row_count - 1, max(groups - 1, 1)
+    dma = pltpu.SemaphoreType.DMA
+    low, wide, whole = jnp.bfloat16, jnp.float32, jnp.int32
+    vmem = pltpu.VMEM
+    return pl.pallas_call(
+        functools.partial(pair_kernel, row_count, ex_count, norm_scale),
+        out_shape=jax.ShapeDtypeStruct((owned, own), low),
+        in_specs=[pl.BlockSpec(memory_space=pltpu.HBM)] * 8,
+        out_specs=pl.BlockSpec(memory_space=pltpu.VMEM),
+        scratch_shapes=[
+            vmem((tok_dev, width), low),
+            vmem((tok_dev, cot_width), low),
+            vmem((1, examples), whole),
+            vmem((1, width), whole),
+            vmem((1, cot_width), whole),
+            vmem((1, features), whole),
+            vmem((1, features), whole),
+            vmem((2, row_count, tok_dev, width), low),
+            vmem((2, tok_dev, cot_width), low),
+            vmem((cot_width, row_count * half), low),
+            vmem((row_count * width, row_count * half), low),
+            vmem((2, tok_dev, row_count * half), wide),
+            vmem((2 * tok_dev, row_count * half), low),
+            vmem((2 * tok_dev, row_count * half), low),
+            vmem((row_count, groups, examples // groups, half), wide),
+            vmem((row_count, others, examples // groups, half), low),
+            vmem((row_count, others, examples // groups, half), low),
+            vmem((last, examples // groups, half), low),
+            vmem((last, examples // groups, half), low),
+            vmem((row_count, 2, owned, own), wide),
+            vmem((row_count, owned, own), wide),
+            vmem((last, owned, own), low),
+            vmem((last, owned, own), low),
+            vmem((row_count, half, own), low),
+            dma((7,)),
+            dma((row_count,)),
+            dma((last,)),
+            dma((last,)),
+            dma((row_count,)),
+            dma((row_count,)),
+            dma,
+            dma,
+            dma((row_count, others)),
+            dma((row_count, others)),
+            dma((last,)),
+            dma((last,)),
+            dma((row_count,)),
+            dma((row_count,)),
+            dma((last,)),
+            dma((last,)),
+        ],
+        compiler_params=pltpu.CompilerParams(
+            collective_id=0, has_side_effects=True, vmem_limit_bytes=48 * 1024 * 1024
+        ),
+        name="features_and_scores",
+    )(*[pltpu.with_memory_space_constraint(operand, pltpu.HBM) for operand in operands])
+
+
 def local(hidden_acts, cotangent, lengths, row_signs, col_signs, feat_row, feat_col, inverse_rows):
     row_count = lax.axis_size("rows")
     ex_count = lax.axis_size("ex")
@@ -328,6 +733,27 @@
     own = features // row_count
     owned = examples // ex_count
     norm_scale = 1.0 / math.sqrt(width * row_count * col_signs.shape[0])
+    operands = (
+        hidden_acts,
+        cotangent,
+        lengths.reshape(1, -1),
+        row_signs.reshape(1, -1),
+        col_signs.reshape(1, -1),
+        feat_row.reshape(1, -1),
+        feat_col.reshape(1, -1),
+        inverse_rows,
+    )
+    if (
+        ex_count % 2 == 0
+        and row_count in (2, 4, 8)
+        and own % 256 == 0
+        and cot_width % 128 == 0
+        and width % 128 == 0
+        and tok_dev % 16 == 0
+        and owned % 8 == 0
+        and features * (width * row_count + cot_width + own) <= 32 * 1024 * 1024
+    ):
+        return pair_call(row_count, ex_count, norm_scale, operands)
     if cot_width % 128 != 0:
         col_signs = lax.dynamic_slice(col_signs, (lax.axis_index("rows") * cot_width,), (cot_width,))
     vmem = pl.BlockSpec(memory_space=pltpu.VMEM)

time: 33.1 us -> 27.7 us (0.84)
  Pallas kernels: 31.5 us -> 26.9 us
  local copies, waits for them, and re-layouts: 1.38 us -> 0.62 us
    pallas_call x1, Pallas kernels: 31.5 us -> 26.9 us  [pair_call(): pl.pallas_call(functools.partial(pair_kernel, row_count, ex_count, norm_s...]
    unnamed x1, local copies, waits for them, and re-layouts: 1.38 us -> 0.62 us
where the time goes in v1:
time: 27.7 us; the launch traced here: 27.6 us
  Pallas kernels  26.9 us (97%)
  local copies, waits for them, and re-layouts  0.62 us (2%)
    pallas_call x1, Pallas kernels, pair_call(): pl.pallas_call(functools.partial(pair_kernel, row_count, ex_count, norm_s...  26.9 us
    unnamed x1, local copies, waits for them, and re-layouts  0.62 us

profile of v1, /device:TPU:0, one launch (start us, length us, event | category | flops | bytes accessed | tf_op | source)
XLA Modules:
  0.0 27.6 jit_solution(6978728108027876456)
XLA Ops:
  0.0 26.9 %features_and_scores.1 = bf16[8,2048]{1,0:T(8,128)(2,1)S(1)} custom-call(bf16[128,128]{1,0:T(8,128)(2,1)} %hid_hbm.1, bf16[128,1024]{1,0:T(8,128)(2,1)} %cot_hbm.1, s32[1,32]{1,0:T(1,128)} %bitcast.8, s32[1,128]{1,0:T(1,128)} %bitcast.9, s32[1,4096]{1,0:T(1,128)} %bitcast.7, s32[1,8192]{1,0:T(1,128)} %bitcast.5, s32[1,8192]{1,0:T(1,128)} %bitcast.6, ...), custom_call_target="tpu_custom_call" | custom-call | tf_op jit(solution)/shard_map/features_and_scores/pallas_call | solution.py:672
  26.9 0.6 %copy.10 = bf16[8,2048]{1,0:T(8,128)(2,1)} copy(bf16[8,2048]{1,0:T(8,128)(2,1)S(1)} %features_and_scores.1) | data formatting | bytes 65536

commit v2 on v1

--- a/solution.py
+++ b/solution.py
@@ -387,11 +387,14 @@
     chunk = min(half, 512)
     mesh_id = pl.DeviceIdType.MESH
     last = row_count - 1
+    masks = sorted(range(row_count), key=lambda m: (m == 0, m != row_count // 2, -m))
+    far = masks.index(last) if row_count == 4 else row_count
+    by_distance = sorted(range(last), key=lambda n: -masks[n])
 
     def other_row(n):
-        far, at = last - n, row
+        at = row
         for bit in range(row_count.bit_length() - 1):
-            if far >> bit & 1:
+            if masks[n] >> bit & 1:
                 at = at + (1 - 2 * lax.rem(row // (1 << bit), 2)) * (1 << bit)
         return at
 
@@ -425,8 +428,11 @@
     for load in loads.values():
         load.start()
 
+    def score_row(n):
+        return row if n == last else n + 1 - jnp.minimum(jnp.maximum(row - n, 0), 1)
+
     def inv_copy(n):
-        target = pl.ds(pl.multiple_of(other_row(n) * own, 128), own)
+        target = pl.ds(pl.multiple_of(score_row(n) * own, 128), own)
         source = pl.ds(pl.multiple_of(core * half, 16), half)
         return pltpu.make_async_copy(inv_ref.at[source, target], inv_buf.at[n], inv_sem.at[n])
 
@@ -441,50 +447,50 @@
 
     loads["hid"].wait()
     loads["rsign"].wait()
-    hid_all[core, row] = hid_buf[...] * rsign_buf[...].astype(jnp.float32).astype(jnp.bfloat16)
+    hid_all[0, last] = hid_buf[...] * rsign_buf[...].astype(jnp.float32).astype(jnp.bfloat16)
     loads["cot"].wait()
     loads["csign"].wait()
-    cot_all[core] = cot_buf[...] * csign_buf[...].astype(jnp.float32).astype(jnp.bfloat16)
+    cot_all[0] = cot_buf[...] * csign_buf[...].astype(jnp.float32).astype(jnp.bfloat16)
     loads["fcol"].wait()
 
     def right_first(i):
         for c in range(half // chunk):
             table = sign_rows(row * cot_width, cot_width // inner, inner, picks_of(fcol_buf, i, c))
             right_table[:, spot(i, c)] = table
-            right_buf[core, :, spot(i, c)] = jnp.dot(
-                cot_all[core], table, preferred_element_type=jnp.float32
+            right_buf[0, :, spot(i, c)] = jnp.dot(
+                cot_all[0], table, preferred_element_type=jnp.float32
             )
 
     def right_mate(i):
         for c in range(half // chunk):
-            right_buf[1 - core, :, spot(i, c)] = jnp.dot(
-                cot_all[1 - core], right_table[:, spot(i, c)], preferred_element_type=jnp.float32
+            right_buf[1, :, spot(i, c)] = jnp.dot(
+                cot_all[1], right_table[:, spot(i, c)], preferred_element_type=jnp.float32
             )
 
-    def hid_copy(n, block):
-        return pltpu.make_async_remote_copy(
-            src_ref=hid_all.at[core, block],
-            dst_ref=hid_all.at[core, block],
+    def hid_copy(n):
+        return pltpu.make_async_remote_copy(
+            src_ref=hid_all.at[0, last],
+            dst_ref=hid_all.at[0, n],
             send_sem=hid_send.at[n],
             recv_sem=hid_recv.at[n],
             device_id={"rows": other_row(n)},
             device_id_type=mesh_id,
         )
 
-    def relay_copy(n, side):
-        return pltpu.make_async_remote_copy(
-            src_ref=hid_all.at[side, other_row(n)],
-            dst_ref=hid_all.at[side, other_row(n)],
+    def relay_copy(n):
+        return pltpu.make_async_remote_copy(
+            src_ref=hid_all.at[0, n],
+            dst_ref=hid_all.at[1, n],
             send_sem=relay_send.at[n],
             recv_sem=relay_recv.at[n],
             device_id={"ex": mate},
             device_id_type=mesh_id,
         )
 
-    def cot_copy(side):
-        return pltpu.make_async_remote_copy(
-            src_ref=cot_all.at[side],
-            dst_ref=cot_all.at[side],
+    def cot_copy():
+        return pltpu.make_async_remote_copy(
+            src_ref=cot_all.at[0],
+            dst_ref=cot_all.at[1],
             send_sem=cot_send,
             recv_sem=cot_recv,
             device_id={"ex": mate},
@@ -495,10 +501,10 @@
     for i in range(early):
         right_first(i)
     pl.semaphore_wait(barrier, last + groups)
-    for n in range(last):
-        hid_copy(n, row).start()
-    relay_copy(last, core).start()
-    cot_copy(core).start()
+    for n in by_distance:
+        hid_copy(n).start()
+    relay_copy(last).start()
+    cot_copy().start()
 
     loads["len"].wait()
     lens = jnp.broadcast_to(len_buf[...].astype(jnp.float32), (examples, examples))
@@ -507,7 +513,9 @@
     ends = jnp.sum(jnp.where(e_col <= e_row, lens, 0.0), axis=1, keepdims=True)
     starts = jnp.sum(jnp.where(e_col < e_row, lens, 0.0), axis=1, keepdims=True)
 
-    spots = 2 * group * tok_dev + lax.broadcasted_iota(jnp.int32, (examples, 2 * tok_dev), 1)
+    spots = lax.broadcasted_iota(jnp.int32, (examples, 2 * tok_dev), 1)
+    mates = (1 - 2 * core) * tok_dev
+    spots = jnp.where(spots < tok_dev, spots, spots - tok_dev + mates) + ex * tok_dev
     spots = spots.astype(jnp.float32)
     member = jnp.where((spots >= starts) & (spots < ends), 1.0, 0.0).astype(jnp.bfloat16)
 
@@ -516,42 +524,50 @@
     loads["frow"].wait()
     for i in range(row_count):
         for c in range(half // chunk):
-            left_table[:, spot(i, c)] = sign_rows(0, row_count, width, picks_of(frow_buf, i, c))
-
-    cot_copy(1 - core).wait_recv()
+            picks = picks_of(frow_buf, i, c)
+            table = signs(lax.broadcasted_iota(jnp.int32, (width, chunk), 0), picks)
+            for n in range(row_count):
+                sign = signs(jnp.zeros_like(picks) + other_row(n) * width, picks)
+                left_table[n * width : (n + 1) * width, spot(i, c)] = table * sign
+
+    cot_copy().wait_recv()
     for i in range(row_count):
         right_mate(i)
 
     for n in range(last):
-        hid_copy(n, other_row(n)).wait_recv()
-        relay_copy(n, core).start()
+        hid_copy(n).wait_recv()
+        relay_copy(n).start()
     for n in range(row_count):
         inv_copy(n).start()
 
-    def products_of(side, tokens):
-        acts = jnp.concatenate([hid_all[side, n] for n in range(row_count)], axis=1)
-        for i in range(row_count):
-            for c in range(half // chunk):
-                left = jnp.dot(acts, left_table[:, spot(i, c)], preferred_element_type=jnp.float32)
-                products = left * right_buf[side, :, spot(i, c)]
-                high = products.astype(jnp.bfloat16)
-                high_buf[tokens, spot(i, c)] = high
-                rest_buf[tokens, spot(i, c)] = (products - high.astype(jnp.float32)).astype(jnp.bfloat16)
-
-    own_tokens = pl.ds(pl.multiple_of(core * tok_dev, 16), tok_dev)
-    mate_tokens = pl.ds(pl.multiple_of((1 - core) * tok_dev, 16), tok_dev)
-    products_of(core, own_tokens)
-    for n in range(row_count):
-        relay_copy(n, 1 - core).wait_recv()
-    products_of(1 - core, mate_tokens)
+    def acts_of(side):
+        return jnp.concatenate([hid_all[side, n] for n in range(row_count)], axis=1)
+
+    def products_of(side, i, acts):
+        tokens = slice(side * tok_dev, (side + 1) * tok_dev)
+        for c in range(half // chunk):
+            left = jnp.dot(acts, left_table[:, spot(i, c)], preferred_element_type=jnp.float32)
+            products = left * right_buf[side, :, spot(i, c)]
+            high = products.astype(jnp.bfloat16)
+            high_buf[tokens, spot(i, c)] = high
+            rest_buf[tokens, spot(i, c)] = (products - high.astype(jnp.float32)).astype(jnp.bfloat16)
+
+    def sums_of(i):
+        at = slice(i * half, (i + 1) * half)
+        sums = jnp.dot(member, high_buf[:, at], preferred_element_type=jnp.float32)
+        sums = sums + jnp.dot(member, rest_buf[:, at], preferred_element_type=jnp.float32)
+        part_buf[i] = sums.reshape(groups, examples // groups, half)
 
     def ex_copy(i, n):
+        to = {"ex": 2 * other_group(n) + core}
+        if i == far:
+            to["rows"] = other_row(i)
         return pltpu.make_async_remote_copy(
             src_ref=ex_out.at[i, n],
             dst_ref=ex_in.at[i, n],
             send_sem=ex_send.at[i, n],
             recv_sem=ex_recv.at[i, n],
-            device_id={"ex": 2 * other_group(n) + core},
+            device_id=to,
             device_id_type=mesh_id,
         )
 
@@ -565,36 +581,45 @@
             device_id_type=mesh_id,
         )
 
-    def sums_of(i):
-        at = slice(i * half, (i + 1) * half)
-        sums = jnp.dot(member, high_buf[:, at], preferred_element_type=jnp.float32)
-        return sums + jnp.dot(member, rest_buf[:, at], preferred_element_type=jnp.float32)
-
-    def ex_start(i, sums):
-        part_buf[i] = sums.reshape(groups, examples // groups, half)
+    def row_start(i, total):
+        row_out[i] = total.astype(row_out.dtype)
+        row_copy(i).start()
+
+    def ex_start(i):
         for n in range(groups - 1):
             ex_out[i, n] = part_buf[i, other_group(n)].astype(ex_out.dtype)
             ex_copy(i, n).start()
-
-    ready = sums_of(0)
-    for i in range(1, row_count):
-        later = sums_of(i)
-        ex_start(i - 1, ready)
-        ready = later
-    ex_start(last, ready)
-
-    total = None
-    for i in range(row_count):
-        total = part_buf[i, group]
+        if i == far:
+            row_start(i, part_buf[i, group])
+
+    def ex_sum(i, total):
         for n in range(groups - 1):
             ex_copy(i, n).wait_recv()
             total = total + ex_in[i, n].astype(jnp.float32)
+        return total
+
+    acts = acts_of(0)
+    for i in range(row_count):
+        products_of(0, i, acts)
+    for n in range(row_count):
+        relay_copy(n).wait_recv()
+    acts = acts_of(1)
+    products_of(1, 0, acts)
+    for i in range(row_count):
         if i < last:
-            row_out[i] = total.astype(row_out.dtype)
-            row_copy(i).start()
-    for n in range(last):
-        row_copy(n).wait_recv()
-        total = total + row_in[n].astype(jnp.float32)
+            products_of(1, i + 1, acts)
+        sums_of(i)
+        ex_start(i)
+
+    for i in range(last):
+        if i != far:
+            row_start(i, ex_sum(i, part_buf[i, group]))
+    total = ex_sum(last, part_buf[last, group])
+    for i in sorted(range(last), key=lambda i: masks[i]):
+        row_copy(i).wait_recv()
+        total = total + row_in[i].astype(jnp.float32)
+        if i == far:
+            total = ex_sum(i, total)
     low = (total * norm_scale).astype(jnp.bfloat16)
 
     def mate_copy(n):
@@ -607,13 +632,13 @@
             device_id_type=mesh_id,
         )
 
-    def score_copy(n):
+    def score_copy(n, slot):
         return pltpu.make_async_remote_copy(
             src_ref=score_out.at[n],
-            dst_ref=score_in.at[n],
+            dst_ref=score_in.at[slot],
             send_sem=score_send.at[n],
-            recv_sem=score_recv.at[n],
-            device_id={"rows": other_row(n)},
+            recv_sem=score_recv.at[slot],
+            device_id={"rows": score_row(n)},
             device_id_type=mesh_id,
         )
 
@@ -636,23 +661,23 @@
         score_block(n)
         if n >= 1:
             score_out[n - 1] = score_sum(n - 1).astype(score_out.dtype)
-            score_copy(n - 1).start()
+            score_copy(n - 1, row - 1 + jnp.minimum(jnp.maximum(score_row(n - 1) - row, 0), 1)).start()
     total = score_sum(last)
     for n in range(last):
-        score_copy(n).wait_recv()
+        score_copy(n, n).wait_recv()
         total = total + score_in[n].astype(jnp.float32)
     out_ref[...] = total.astype(out_ref.dtype)
 
-    cot_copy(core).wait_send()
+    cot_copy().wait_send()
     for n in range(row_count):
-        relay_copy(n, core).wait_send()
+        relay_copy(n).wait_send()
         mate_copy(n).wait_send()
         for m in range(groups - 1):
             ex_copy(n, m).wait_send()
     for n in range(last):
-        hid_copy(n, row).wait_send()
+        hid_copy(n).wait_send()
         row_copy(n).wait_send()
-        score_copy(n).wait_send()
+        score_copy(n, n).wait_send()
 
 
 def pair_call(row_count, ex_count, norm_scale, operands):

time: 27.7 us -> 25.7 us (0.928)
  Pallas kernels: 26.9 us -> 24.9 us
    pallas_call x1, Pallas kernels: 26.9 us -> 24.9 us  [pair_call(): pl.pallas_call(functools.partial(pair_kernel, row_count, ex_count, norm_s...]
where the time goes in v2:
time: 25.7 us; the launch traced here: 25.5 us
  Pallas kernels  24.9 us (97%)
  local copies, waits for them, and re-layouts  0.62 us (2%)
    pallas_call x1, Pallas kernels, pair_call(): pl.pallas_call(functools.partial(pair_kernel, row_count, ex_count, norm_s...  24.9 us
    unnamed x1, local copies, waits for them, and re-layouts  0.62 us

profile of v2, /device:TPU:0, one launch (start us, length us, event | category | flops | bytes accessed | tf_op | source)
XLA Modules:
  0.0 25.5 jit_solution(14996214007715386046)
XLA Ops:
  0.0 24.9 %features_and_scores.1 = bf16[8,2048]{1,0:T(8,128)(2,1)S(1)} custom-call(bf16[128,128]{1,0:T(8,128)(2,1)} %hid_hbm.1, bf16[128,1024]{1,0:T(8,128)(2,1)} %cot_hbm.1, s32[1,32]{1,0:T(1,128)} %bitcast.8, s32[1,128]{1,0:T(1,128)} %bitcast.9, s32[1,4096]{1,0:T(1,128)} %bitcast.7, s32[1,8192]{1,0:T(1,128)} %bitcast.5, s32[1,8192]{1,0:T(1,128)} %bitcast.6, ...), custom_call_target="tpu_custom_call" | custom-call | tf_op jit(solution)/shard_map/features_and_scores/pallas_call | solution.py:697
  24.9 0.6 %copy.10 = bf16[8,2048]{1,0:T(8,128)(2,1)} copy(bf16[8,2048]{1,0:T(8,128)(2,1)S(1)} %features_and_scores.1) | data formatting | bytes 65536

commit v3 on v2

--- a/solution.py
+++ b/solution.py
@@ -340,7 +340,6 @@
     fcol_buf,
     hid_all,
     cot_all,
-    right_table,
     left_table,
     right_buf,
     high_buf,
@@ -348,6 +347,8 @@
     part_buf,
     ex_out,
     ex_in,
+    cross_in,
+    total_buf,
     row_out,
     row_in,
     keep_buf,
@@ -365,6 +366,8 @@
     cot_recv,
     ex_send,
     ex_recv,
+    cross_send,
+    cross_recv,
     row_send,
     row_recv,
     mate_send,
@@ -387,16 +390,28 @@
     chunk = min(half, 512)
     mesh_id = pl.DeviceIdType.MESH
     last = row_count - 1
-    masks = sorted(range(row_count), key=lambda m: (m == 0, m != row_count // 2, -m))
-    far = masks.index(last) if row_count == 4 else row_count
-    by_distance = sorted(range(last), key=lambda n: -masks[n])
-
-    def other_row(n):
+    four = row_count == 4
+    inside = lax.rem(row + 1, 4) // 2 if four else 1
+    orders = ((3, 2, 1, 0), (2, 3, 1, 0)) if four else (tuple(range(last, -1, -1)),) * 2
+
+    def pick(outer, inner):
+        return outer + inside * (inner - outer)
+
+    def flip(mask):
         at = row
         for bit in range(row_count.bit_length() - 1):
-            if masks[n] >> bit & 1:
+            if mask >> bit & 1:
                 at = at + (1 - 2 * lax.rem(row // (1 << bit), 2)) * (1 << bit)
         return at
+
+    def other_row(n):
+        outer, inner = orders[0][n], orders[1][n]
+        return flip(outer) if outer == inner else pick(flip(outer), flip(inner))
+
+    def slot_there(n):
+        if not four:
+            return n
+        return pick(orders[1 if orders[0][n] < last else 0].index(orders[0][n]), orders[0 if orders[1][n] < last else 1].index(orders[1][n]))
 
     def other_group(n):
         return lax.rem(group + 1 + n, groups)
@@ -443,8 +458,6 @@
     def spot(i, c):
         return slice(i * half + c * chunk, i * half + (c + 1) * chunk)
 
-    inner = min(cot_width, 128)
-
     loads["hid"].wait()
     loads["rsign"].wait()
     hid_all[0, last] = hid_buf[...] * rsign_buf[...].astype(jnp.float32).astype(jnp.bfloat16)
@@ -453,10 +466,19 @@
     cot_all[0] = cot_buf[...] * csign_buf[...].astype(jnp.float32).astype(jnp.bfloat16)
     loads["fcol"].wait()
 
+    def short_rows(first, rows, picks):
+        step = min(rows, 16)
+        table = signs(lax.broadcasted_iota(jnp.int32, (step, chunk), 0), picks)
+        table = table * signs(jnp.zeros_like(picks) + first, picks)
+        blocks = signs(lax.broadcasted_iota(jnp.int32, (rows // step, chunk), 0) * step, picks)
+        return jnp.concatenate([table * blocks[n : n + 1] for n in range(rows // step)], axis=0)
+
+    def table_of(i, c):
+        return short_rows(row * cot_width, cot_width, picks_of(fcol_buf, i, c))
+
     def right_first(i):
         for c in range(half // chunk):
-            table = sign_rows(row * cot_width, cot_width // inner, inner, picks_of(fcol_buf, i, c))
-            right_table[:, spot(i, c)] = table
+            table = table_of(i, c)
             right_buf[0, :, spot(i, c)] = jnp.dot(
                 cot_all[0], table, preferred_element_type=jnp.float32
             )
@@ -464,15 +486,15 @@
     def right_mate(i):
         for c in range(half // chunk):
             right_buf[1, :, spot(i, c)] = jnp.dot(
-                cot_all[1], right_table[:, spot(i, c)], preferred_element_type=jnp.float32
+                cot_all[1], table_of(i, c), preferred_element_type=jnp.float32
             )
 
-    def hid_copy(n):
+    def hid_copy(n, slot):
         return pltpu.make_async_remote_copy(
             src_ref=hid_all.at[0, last],
-            dst_ref=hid_all.at[0, n],
+            dst_ref=hid_all.at[0, slot],
             send_sem=hid_send.at[n],
-            recv_sem=hid_recv.at[n],
+            recv_sem=hid_recv.at[slot],
             device_id={"rows": other_row(n)},
             device_id_type=mesh_id,
         )
@@ -501,8 +523,8 @@
     for i in range(early):
         right_first(i)
     pl.semaphore_wait(barrier, last + groups)
-    for n in by_distance:
-        hid_copy(n).start()
+    for n in range(last):
+        hid_copy(n, slot_there(n)).start()
     relay_copy(last).start()
     cot_copy().start()
 
@@ -525,17 +547,16 @@
     for i in range(row_count):
         for c in range(half // chunk):
             picks = picks_of(frow_buf, i, c)
-            table = signs(lax.broadcasted_iota(jnp.int32, (width, chunk), 0), picks)
             for n in range(row_count):
-                sign = signs(jnp.zeros_like(picks) + other_row(n) * width, picks)
-                left_table[n * width : (n + 1) * width, spot(i, c)] = table * sign
+                rows = slice(n * width, (n + 1) * width)
+                left_table[rows, spot(i, c)] = short_rows(other_row(n) * width, width, picks)
 
     cot_copy().wait_recv()
     for i in range(row_count):
         right_mate(i)
 
     for n in range(last):
-        hid_copy(n).wait_recv()
+        hid_copy(n, n).wait_recv()
         relay_copy(n).start()
     for n in range(row_count):
         inv_copy(n).start()
@@ -559,38 +580,62 @@
         part_buf[i] = sums.reshape(groups, examples // groups, half)
 
     def ex_copy(i, n):
-        to = {"ex": 2 * other_group(n) + core}
-        if i == far:
-            to["rows"] = other_row(i)
         return pltpu.make_async_remote_copy(
             src_ref=ex_out.at[i, n],
             dst_ref=ex_in.at[i, n],
             send_sem=ex_send.at[i, n],
             recv_sem=ex_recv.at[i, n],
-            device_id=to,
+            device_id={"ex": 2 * other_group(n) + core},
             device_id_type=mesh_id,
         )
 
-    def row_copy(i):
+    def cross_copy(i, n, slot):
+        return pltpu.make_async_remote_copy(
+            src_ref=ex_out.at[i, n],
+            dst_ref=cross_in.at[slot, n],
+            send_sem=cross_send.at[i, n],
+            recv_sem=cross_recv.at[slot, n],
+            device_id={"rows": other_row(i), "ex": 2 * other_group(n) + core},
+            device_id_type=mesh_id,
+        )
+
+    def when_inside(is_inside, body):
+        if four:
+            pl.when(inside == is_inside)(body)
+        elif is_inside:
+            body()
+
+    def row_copy(i, slot):
         return pltpu.make_async_remote_copy(
             src_ref=row_out.at[i],
-            dst_ref=row_in.at[i],
+            dst_ref=row_in.at[slot],
             send_sem=row_send.at[i],
-            recv_sem=row_recv.at[i],
+            recv_sem=row_recv.at[slot],
             device_id={"rows": other_row(i)},
             device_id_type=mesh_id,
         )
 
     def row_start(i, total):
         row_out[i] = total.astype(row_out.dtype)
-        row_copy(i).start()
+        row_copy(i, slot_there(i)).start()
+
+    def two_phase(i):
+        for n in range(groups - 1):
+            ex_copy(i, n).start()
+
+    def one_phase(i):
+        for n in range(groups - 1):
+            cross_copy(i, n, slot_there(i)).start()
+        row_start(i, part_buf[i, group])
 
     def ex_start(i):
         for n in range(groups - 1):
             ex_out[i, n] = part_buf[i, other_group(n)].astype(ex_out.dtype)
-            ex_copy(i, n).start()
-        if i == far:
-            row_start(i, part_buf[i, group])
+        if i == last:
+            two_phase(i)
+        else:
+            when_inside(1, lambda: two_phase(i))
+            when_inside(0, lambda: one_phase(i))
 
     def ex_sum(i, total):
         for n in range(groups - 1):
@@ -604,23 +649,31 @@
     for n in range(row_count):
         relay_copy(n).wait_recv()
     acts = acts_of(1)
-    products_of(1, 0, acts)
     for i in range(row_count):
-        if i < last:
-            products_of(1, i + 1, acts)
+        products_of(1, i, acts)
         sums_of(i)
         ex_start(i)
 
-    for i in range(last):
-        if i != far:
+    def pass_on():
+        for i in range(last):
             row_start(i, ex_sum(i, part_buf[i, group]))
-    total = ex_sum(last, part_buf[last, group])
-    for i in sorted(range(last), key=lambda i: masks[i]):
-        row_copy(i).wait_recv()
-        total = total + row_in[i].astype(jnp.float32)
-        if i == far:
-            total = ex_sum(i, total)
-    low = (total * norm_scale).astype(jnp.bfloat16)
+
+    when_inside(1, pass_on)
+    total_buf[...] = ex_sum(last, part_buf[last, group])
+    for i in reversed(range(last)):
+        row_copy(i, i).wait_recv()
+        total_buf[...] = total_buf[...] + row_in[i].astype(jnp.float32)
+
+        def add_cross(i=i):
+            for n in range(groups - 1):
+                cross_copy(i, n, i).wait_recv()
+                total_buf[...] = total_buf[...] + cross_in[i, n].astype(jnp.float32)
+
+        if four and i == 0:
+            add_cross()
+        elif four and i == 2:
+            when_inside(1, add_cross)
+    low = (total_buf[...] * norm_scale).astype(jnp.bfloat16)
 
     def mate_copy(n):
         return pltpu.make_async_remote_copy(
@@ -673,10 +726,14 @@
         relay_copy(n).wait_send()
         mate_copy(n).wait_send()
         for m in range(groups - 1):
-            ex_copy(n, m).wait_send()
+            if n == last:
+                ex_copy(n, m).wait_send()
+            else:
+                when_inside(1, ex_copy(n, m).wait_send)
+                when_inside(0, cross_copy(n, m, n).wait_send)
     for n in range(last):
-        hid_copy(n).wait_send()
-        row_copy(n).wait_send()
+        hid_copy(n, n).wait_send()
+        row_copy(n, n).wait_send()
         score_copy(n, n).wait_send()
 
 
@@ -709,7 +766,6 @@
             vmem((1, features), whole),
             vmem((2, row_count, tok_dev, width), low),
             vmem((2, tok_dev, cot_width), low),
-            vmem((cot_width, row_count * half), low),
             vmem((row_count * width, row_count * half), low),
             vmem((2, tok_dev, row_count * half), wide),
             vmem((2 * tok_dev, row_count * half), low),
@@ -717,6 +773,8 @@
             vmem((row_count, groups, examples // groups, half), wide),
             vmem((row_count, others, examples // groups, half), low),
             vmem((row_count, others, examples // groups, half), low),
+            vmem((last, others, examples // groups, half), low),
+            vmem((examples // groups, half), wide),
             vmem((last, examples // groups, half), low),
             vmem((last, examples // groups, half), low),
             vmem((row_count, 2, owned, own), wide),
@@ -734,6 +792,8 @@
             dma,
             dma((row_count, others)),
             dma((row_count, others)),
+            dma((last, others)),
+            dma((last, others)),
             dma((last,)),
             dma((last,)),
             dma((row_count,)),

time: 25.7 us -> 25.3 us (0.984)
  Pallas kernels: 24.9 us -> 24.6 us
    pallas_call x1, Pallas kernels: 24.9 us -> 24.6 us  [pair_call(): pl.pallas_call(functools.partial(pair_kernel, row_count, ex_count, norm_s...]
where the time goes in v3:
time: 25.3 us; the launch traced here: 25.2 us
  Pallas kernels  24.6 us (97%)
  local copies, waits for them, and re-layouts  0.62 us (2%)
    pallas_call x1, Pallas kernels, pair_call(): pl.pallas_call(functools.partial(pair_kernel, row_count, ex_count, norm_s...  24.6 us
    unnamed x1, local copies, waits for them, and re-layouts  0.62 us

profile of v3, /device:TPU:0, one launch (start us, length us, event | category | flops | bytes accessed | tf_op | source)
XLA Modules:
  0.0 25.2 jit_solution(6487500804152429811)
XLA Ops:
  0.0 24.6 %features_and_scores.1 = bf16[8,2048]{1,0:T(8,128)(2,1)S(1)} custom-call(bf16[128,128]{1,0:T(8,128)(2,1)} %hid_hbm.1, bf16[128,1024]{1,0:T(8,128)(2,1)} %cot_hbm.1, s32[1,32]{1,0:T(1,128)} %bitcast.8, s32[1,128]{1,0:T(1,128)} %bitcast.9, s32[1,4096]{1,0:T(1,128)} %bitcast.7, s32[1,8192]{1,0:T(1,128)} %bitcast.5, s32[1,8192]{1,0:T(1,128)} %bitcast.6, ...), custom_call_target="tpu_custom_call" | custom-call | tf_op jit(solution)/shard_map/features_and_scores/pallas_call | solution.py:754
  24.6 0.6 %copy.10 = bf16[8,2048]{1,0:T(8,128)(2,1)} copy(bf16[8,2048]{1,0:T(8,128)(2,1)S(1)} %features_and_scores.1) | data formatting | bytes 65536

commit v4 on v3

--- a/solution.py
+++ b/solution.py
@@ -519,13 +519,17 @@
             device_id_type=mesh_id,
         )
 
+    def enter():
+        pl.semaphore_wait(barrier, last + groups)
+        for n in range(last):
+            hid_copy(n, slot_there(n)).start()
+        relay_copy(last).start()
+
+    pl.when(row == last)(enter)
     early = row_count // 2
     for i in range(early):
         right_first(i)
-    pl.semaphore_wait(barrier, last + groups)
-    for n in range(last):
-        hid_copy(n, slot_there(n)).start()
-    relay_copy(last).start()
+    pl.when(row < last)(enter)
     cot_copy().start()
 
     loads["len"].wait()

time: 25.3 us -> 25.3 us (level)
  no operation moved by 1% of the time
where the time goes in v4:
time: 25.3 us; the launch traced here: 25.2 us
  Pallas kernels  24.6 us (97%)
  local copies, waits for them, and re-layouts  0.62 us (2%)
    pallas_call x1, Pallas kernels, pair_call(): pl.pallas_call(functools.partial(pair_kernel, row_count, ex_count, norm_s...  24.6 us
    unnamed x1, local copies, waits for them, and re-layouts  0.62 us

profile of v4, /device:TPU:0, one launch (start us, length us, event | category | flops | bytes accessed | tf_op | source)
XLA Modules:
  0.0 25.2 jit_solution(6093107672432445445)
XLA Ops:
  0.0 24.6 %features_and_scores.1 = bf16[8,2048]{1,0:T(8,128)(2,1)S(1)} custom-call(bf16[128,128]{1,0:T(8,128)(2,1)} %hid_hbm.1, bf16[128,1024]{1,0:T(8,128)(2,1)} %cot_hbm.1, s32[1,32]{1,0:T(1,128)} %bitcast.8, s32[1,128]{1,0:T(1,128)} %bitcast.9, s32[1,4096]{1,0:T(1,128)} %bitcast.7, s32[1,8192]{1,0:T(1,128)} %bitcast.5, s32[1,8192]{1,0:T(1,128)} %bitcast.6, ...), custom_call_target="tpu_custom_call" | custom-call | tf_op jit(solution)/shard_map/features_and_scores/pallas_call | solution.py:758
  24.6 0.6 %copy.10 = bf16[8,2048]{1,0:T(8,128)(2,1)} copy(bf16[8,2048]{1,0:T(8,128)(2,1)S(1)} %features_and_scores.1) | data formatting | bytes 65536

commit v5 on v3

--- a/solution.py
+++ b/solution.py
@@ -387,7 +387,7 @@
     own = features // row_count
     half = own // 2
     examples = len_hbm.shape[1]
-    chunk = min(half, 512)
+    chunk = min(half, 1024)
     mesh_id = pl.DeviceIdType.MESH
     last = row_count - 1
     four = row_count == 4

time: 25.3 us -> 25.3 us (level)
  no operation moved by 1% of the time
where the time goes in v5:
time: 25.3 us; the launch traced here: 25.2 us
  Pallas kernels  24.6 us (97%)
  local copies, waits for them, and re-layouts  0.62 us (2%)
    pallas_call x1, Pallas kernels, pair_call(): pl.pallas_call(functools.partial(pair_kernel, row_count, ex_count, norm_s...  24.6 us
    unnamed x1, local copies, waits for them, and re-layouts  0.62 us

profile of v5, /device:TPU:0, one launch (start us, length us, event | category | flops | bytes accessed | tf_op | source)
XLA Modules:
  0.0 25.2 jit_solution(13986280740871402450)
XLA Ops:
  0.0 24.6 %features_and_scores.1 = bf16[8,2048]{1,0:T(8,128)(2,1)S(1)} custom-call(bf16[128,128]{1,0:T(8,128)(2,1)} %hid_hbm.1, bf16[128,1024]{1,0:T(8,128)(2,1)} %cot_hbm.1, s32[1,32]{1,0:T(1,128)} %bitcast.8, s32[1,128]{1,0:T(1,128)} %bitcast.9, s32[1,4096]{1,0:T(1,128)} %bitcast.7, s32[1,8192]{1,0:T(1,128)} %bitcast.5, s32[1,8192]{1,0:T(1,128)} %bitcast.6, ...), custom_call_target="tpu_custom_call" | custom-call | tf_op jit(solution)/shard_map/features_and_scores/pallas_call | solution.py:754
  24.6 0.6 %copy.10 = bf16[8,2048]{1,0:T(8,128)(2,1)} copy(bf16[8,2048]{1,0:T(8,128)(2,1)S(1)} %features_and_scores.1) | data formatting | bytes 65536
